TPU v7x, 256 devices: a whole 4x4x8 slice. The times are simulated.
256 devices in a mesh: hid: 128 (over x, z, y), seq: 2 (over core).
Axes of the slice: x: 4, y: 4, z: 8, core: 2. Of those that a mesh axis runs over, the one named last changes fastest.
Arguments:
- pre_act: bfloat16 [1536, 32768], P(('hid', 'seq')), may hold values from -6 to 6
- butterfly: bfloat16 [128, 5, 256, 256], P('hid'), may hold values from -0.15625 to 0.15625
- low_u: bfloat16 [32768, 256], P('hid'), may hold values from -0.25 to 0.25
- low_v: bfloat16 [256, 32768], P(None, 'hid'), may hold values from -0.0625 to 0.0625
- grad_out: bfloat16 [1536, 32768], P(('hid', 'seq')), may hold values from -6 to 6
Outputs:
- output: bfloat16 [1536, 32768], P(('hid', 'seq'))
- grad_pre: bfloat16 [1536, 32768], P(('hid', 'seq'))
- grad_butterfly: float32 [128, 5, 256, 256], P('hid', None, 'seq')
- grad_low_u: float32 [32768, 256], P('hid', 'seq')
- grad_low_v: float32 [256, 32768], P('seq', 'hid')
All inputs are finite; a program needn't handle non-finite values.
Results may differ from a plain program's by a relative error of at most 0.0075.
Values may be sent and summed in bfloat16 or wider, within the bound.
A program may use at most 64 MiB of HBM per device.

v0:
```python
import math
import jax
import jax.numpy as jnp
from jax import lax
from jax.sharding import PartitionSpec as P

LEVELS = 4


def swapped(x, axis, stride):
    return lax.ppermute(x, axis, [(i, i ^ 1 << stride) for i in range(lax.axis_size(axis))])


def gelu_tanh(value):
    return jax.nn.gelu(value, approximate=True)


def reduce_latents(first, second):
    both = jnp.concatenate([first, second], axis=1)
    rows, wide = both.shape
    flat = both.reshape(rows * wide // 128, 128)
    part = lax.psum_scatter(flat, "hid", scatter_dimension=0, tiled=True)
    full = lax.all_gather(part.astype(jnp.bfloat16), "hid", axis=0, tiled=True)
    full = full.reshape(rows, wide)
    return (full[:, : wide // 2], full[:, wide // 2 :])


def inner_rows(left, right):
    return lax.dot_general(
        left, right, (((0,), (0,)), ((), ())), preferred_element_type=jnp.float32
    )


def on_device(pre_act, butterfly, low_u, low_v, grad_out):
    pre_f = pre_act.astype(jnp.float32)
    act_tok = gelu_tanh(pre_f).astype(jnp.bfloat16)
    act_rows = lax.all_to_all(act_tok, "hid", split_axis=1, concat_axis=0, tiled=True)
    partners = [act_rows]
    for level in range(LEVELS):
        partners.append(swapped(act_rows, "hid", level))
    grad_rows = lax.all_to_all(grad_out, "hid", split_axis=1, concat_axis=0, tiled=True)
    latent, dlatent = reduce_latents(
        jnp.dot(act_rows, low_u, preferred_element_type=jnp.float32),
        jnp.dot(grad_rows, low_v.T, preferred_element_type=jnp.float32),
    )
    total = jnp.dot(latent, low_v, preferred_element_type=jnp.float32)
    for level in range(LEVELS + 1):
        total = total + jnp.dot(
            partners[level], butterfly[0, level], preferred_element_type=jnp.float32
        )
    output_rows = total.astype(jnp.bfloat16)
    output_tok = lax.all_to_all(output_rows, "hid", split_axis=0, concat_axis=1, tiled=True)
    backward = jnp.dot(dlatent, low_u.T, preferred_element_type=jnp.float32)
    backward = backward + jnp.dot(grad_rows, butterfly[0, 0].T, preferred_element_type=jnp.float32)
    for level in range(1, LEVELS + 1):
        grad_far, weight_far = swapped((grad_rows, butterfly[0, level]), "hid", level - 1)
        backward = backward + jnp.dot(grad_far, weight_far.T, preferred_element_type=jnp.float32)
    grad_act = backward.astype(jnp.bfloat16)
    tokens_all = pre_act.shape[0] * lax.axis_size("hid") * lax.axis_size("seq")
    factor = 1.0 / math.sqrt(tokens_all)
    block_grads = jnp.stack(
        [inner_rows(partners[level], grad_rows) for level in range(LEVELS + 1)], axis=0
    )
    block_grads = block_grads[None] * factor
    low_u_grad = inner_rows(act_rows, dlatent) * factor
    low_v_grad = inner_rows(latent, grad_rows) * factor
    grad_butterfly, grad_low_u, grad_low_v = (
        lax.psum_scatter(
            block_grads.astype(jnp.bfloat16), "seq", scatter_dimension=2, tiled=True
        ).astype(jnp.float32),
        lax.psum_scatter(
            low_u_grad.astype(jnp.bfloat16), "seq", scatter_dimension=1, tiled=True
        ).astype(jnp.float32),
        lax.psum_scatter(
            low_v_grad.astype(jnp.bfloat16), "seq", scatter_dimension=0, tiled=True
        ).astype(jnp.float32),
    )
    grad_act_tok = lax.all_to_all(grad_act, "hid", split_axis=0, concat_axis=1, tiled=True)
    unused, pullback = jax.vjp(gelu_tanh, pre_f)
    grad_pre = pullback(grad_act_tok.astype(jnp.float32))[0].astype(jnp.bfloat16)
    return (output_tok, grad_pre, grad_butterfly, grad_low_u, grad_low_v)


def solution(mesh):
    in_specs = (
        P(("hid", "seq"), None),
        P("hid", None, None, None),
        P("hid", None),
        P(None, "hid"),
        P(("hid", "seq"), None),
    )
    out_specs = (
        P(("hid", "seq"), None),
        P(("hid", "seq"), None),
        P("hid", None, "seq", None),
        P("hid", "seq"),
        P("seq", "hid"),
    )
    return jax.shard_map(
        on_device, mesh=mesh, in_specs=in_specs, out_specs=out_specs, check_vma=False
    )
```

profile of v0, /device:TPU:32, one launch (start us, length us, event | category | flops | bytes accessed | tf_op | source)
XLA Modules:
  0.0 1346.6 jit_solution(5480149929187112660)
XLA Ops:
  7.2 1.4 fusion.22
  8.6 33.9 %all_to_all.70 = bf16[6,128,256]{2,0,1:T(8,128)(2,1)S(1)} all-to-all(bf16[6,128,256]{2,0,1:T(8,128)(2,1)S(1)} %bitcast.92), channel_id=1, replica_groups=mesh['hid'=128,'seq'=2] {'hid'}, dimensions={1} | all-to-all | bytes 786432 | tf_op jit(solution)/shard_map/all_to_all | solution.py:37
  42.5 7.2 all-to-all-start.1
  49.8 0.1 all_to_all.55
  49.9 1.6 collective-permute-start
  51.5 2.7 collective-permute-start.1
  54.2 0.6 collective-permute-start.2
  54.7 2.4 collective-permute-start.3
  57.1 21.0 %all-to-all-done.1 = bf16[6,128,256]{2,0,1:T(8,128)(2,1)S(1)} async-done(((bf16[6,128,256]{2,0,1:T(8,128)(2,1)}), bf16[6,128,256]{2,0,1:T(8,128)(2,1)S(1)}, u32[]{:S(2)}, u32[]{:S(2)}) %all-to-all-start.1) | async-done | bytes 393248 | tf_op jit(solution)/shard_map/all_to_all | solution.py:41
  78.1 0.1 all_to_all.59
  78.2 1.1 copy.15
  79.3 1.3 fusion.13
  80.6 1.3 fusion.12
  81.9 0.3 fusion.11
  82.2 0.3 fusion.10
  82.6 0.3 fusion.9
  82.9 1.0 multiply_convert_fusion
  84.0 0.3 fusion.42
  84.3 0.3 fusion.41
  84.7 1.6 copy.19
  86.3 2.5 reshape.108
  88.9 1.0 copy-done.4
  89.9 0.7 slice_bitcast_fusion.3
  90.6 0.9 collective-permute-start.7
  91.4 0.3 collective-permute-start.9
  91.7 1.8 collective-permute-start.11
  93.5 1.4 collective-permute-start.6
  94.9 2.0 collective-permute-start.8
  97.0 0.2 fusion.38
  97.2 1.2 fusion.39
  98.4 1.2 fusion.40
  99.6 0.6 collective-permute-start.5
  100.2 4.8 collective-permute-done.6
  105.0 0.5 collective-permute-start.10
  105.5 1.2 fusion.43
  106.8 1.0 collective-permute-start.4
  107.7 1.2 fusion.44
  108.9 8.4 collective-permute-done.10
  117.3 1.2 fusion.45
  118.5 1.9 convert_element_type.63
  120.4 801.2 %reduce-scatter.15.cloned.1.call-done = f32[24,128]{1,0:T(8,128)} async-done(((f32[3072,128]{1,0:T(8,128)}), f32[24,128]{1,0:T(8,128)}) %reduce-scatter.15.cloned.1.call-update) | async-done | bytes 12304
  921.6 0.7 convert_element_type.55
  922.3 337.9 %all_gather.3 = bf16[3072,128]{1,0:T(8,128)(2,1)S(1)} all-gather(bf16[24,128]{1,0:T(8,128)(2,1)S(1)} %convert_element_type.55), channel_id=1, replica_groups=mesh['hid'=128,'seq'=2] {'hid'}, dimensions={0}, use_global_device_ids=true | all-gather | bytes 792576 | tf_op jit(solution)/shard_map/all_gather | solution.py:23
  1260.1 0.5 reshape.109
  1260.6 0.3 fusion.29
  1260.9 2.1 convolution_add_fusion.1
  1263.0 1.0 fusion.14
  1264.0 1.7 copy.22
  1265.7 2.8 fusion.8
  1268.5 1.9 all_to_all.64
  1270.4 16.0 %all-to-all-start.3 = ((bf16[128,6,256]{2,1,0:T(8,128)(2,1)}), bf16[128,6,256]{2,1,0:T(8,128)(2,1)S(1)}, u32[]{:S(2)}, u32[]{:S(2)}) async-start(bf16[128,6,256]{2,1,0:T(8,128)(2,1)} %all_to_all.64), calls=%async_computation.3 | async-start | bytes 1048576 | tf_op jit(solution)/shard_map/all_to_all | solution.py:78
  1286.5 1.0 fusion.15
  1287.5 0.3 fusion.32
  1287.8 1.3 convolution_add_fusion.3
  1289.2 1.3 fusion.7
  1290.5 0.9 all_to_all.60
  1291.4 0.9 copy.23
  1292.4 0.7 convert_element_type.65
  1293.1 11.3 reduce-scatter.11.cloned.1.call-done
  1304.4 1.5 convert_element_type.67
  1305.9 13.8 %all-to-all-start.2 = ((bf16[128,6,256]{2,1,0:T(8,128)(2,1)}), bf16[128,6,256]{2,1,0:T(8,128)(2,1)S(1)}, u32[]{:S(2)}, u32[]{:S(2)}) async-start(bf16[128,6,256]{2,1,0:T(8,128)(2,1)} %all_to_all.60), calls=%async_computation.2 | async-start | bytes 1048576 | tf_op jit(solution)/shard_map/all_to_all | solution.py:52
  1319.8 1.5 fusion.18
  1321.3 18.0 %all-to-all-done.2 = bf16[128,6,256]{2,1,0:T(8,128)(2,1)S(1)} async-done(((bf16[128,6,256]{2,1,0:T(8,128)(2,1)}), bf16[128,6,256]{2,1,0:T(8,128)(2,1)S(1)}, u32[]{:S(2)}, u32[]{:S(2)}) %all-to-all-start.2) | async-done | bytes 393248 | tf_op jit(solution)/shard_map/all_to_all | solution.py:52
  1339.3 0.8 copy.33
  (40 shorter events, 0.6 us)
Async XLA Ops:
  7.2 77.1 %copy-start = (bf16[256,256]{1,0:T(8,128)(2,1)S(1)}, bf16[256,256]{1,0:T(8,128)(2,1)}, u32[]{:S(2)}) copy-start(bf16[256,256]{1,0:T(8,128)(2,1)} %param.7) | copy-start | bytes 393220
  42.5 35.5 %all-to-all-start.1 = ((bf16[6,128,256]{2,0,1:T(8,128)(2,1)}), bf16[6,128,256]{2,0,1:T(8,128)(2,1)S(1)}, u32[]{:S(2)}, u32[]{:S(2)}) async-start(bf16[6,128,256]{2,0,1:T(8,128)(2,1)} %bitcast.3), calls=%async_computation.1 | async-start | bytes 1048576 | tf_op jit(solution)/shard_map/all_to_all | solution.py:41
  49.7 68.8 %reduce-scatter.9.cloned.1.call-start = ((), (), s32[]{:S(2)}) async-start(), calls=%async_computation.8 | async-start | bytes 983040 | tf_op jit(solution)/shard_map/reduce_scatter | solution.py:68
  49.9 30.6 %collective-permute-start = (bf16[768,256]{1,0:T(8,128)(2,1)S(1)}, bf16[768,256]{1,0:T(8,128)(2,1)}, u32[]{:S(2)}, u32[]{:S(2)}) collective-permute-start(bf16[768,256]{1,0:T(8,128)(2,1)S(1)} %all_to_all.55), channel_id=1, source_target_pairs={{0,2},{2,0},{4,6},{6,4},{8,10},{10,8},{12,14},{14,12},{16,18},{18,... | collective-permute-start | bytes 1179656 | tf_op jit(solution)/shard_map/ppermute | solution.py:11
  51.5 30.4 %collective-permute-start.1 = (bf16[768,256]{1,0:T(8,128)(2,1)S(1)}, bf16[768,256]{1,0:T(8,128)(2,1)S(1)}, u32[]{:S(2)}, u32[]{:S(2)}) collective-permute-start(bf16[768,256]{1,0:T(8,128)(2,1)S(1)} %all_to_all.55), channel_id=1, source_target_pairs={{0,4},{2,6},{4,0},{6,2},{8,12},{10,14},{12,8},{14,10},{16,20},{18,... | collective-permute-start | bytes 1179656 | tf_op jit(solution)/shard_map/ppermute | solution.py:11
  54.2 28.1 %collective-permute-start.2 = (bf16[768,256]{1,0:T(8,128)(2,1)S(1)}, bf16[768,256]{1,0:T(8,128)(2,1)S(1)}, u32[]{:S(2)}, u32[]{:S(2)}) collective-permute-start(bf16[768,256]{1,0:T(8,128)(2,1)S(1)} %all_to_all.55), channel_id=1, source_target_pairs={{0,8},{2,10},{4,12},{6,14},{8,0},{10,2},{12,4},{14,6},{16,24},{18,... | collective-permute-start | bytes 1179656 | tf_op jit(solution)/shard_map/ppermute | solution.py:11
  54.7 27.8 %collective-permute-start.3 = (bf16[768,256]{1,0:T(8,128)(2,1)S(1)}, bf16[768,256]{1,0:T(8,128)(2,1)S(1)}, u32[]{:S(2)}, u32[]{:S(2)}) collective-permute-start(bf16[768,256]{1,0:T(8,128)(2,1)S(1)} %all_to_all.55), channel_id=1, source_target_pairs={{0,16},{2,18},{4,20},{6,22},{8,24},{10,26},{12,28},{14,30},{16,0},... | collective-permute-start | bytes 1179656 | tf_op jit(solution)/shard_map/ppermute | solution.py:11
  82.6 1.3 copy-start.6
  82.9 1.1 copy-start.8
  83.9 837.7 %reduce-scatter.15.cloned.1.call-start = ((), (), s32[]{:S(2)}) async-start(), calls=%async_computation.11 | async-start | bytes 1585152
  88.8 1.1 copy-start.4
  88.8 1202.6 %reduce-scatter.13.cloned.1.call-start = ((), (), s32[]{:S(2)}) async-start(), calls=%async_computation.10 | async-start | bytes 196608
  90.6 9.0 collective-permute-start.7
  91.4 15.3 %collective-permute-start.9 = (bf16[256,256]{1,0:T(8,128)(2,1)S(1)}, bf16[256,256]{1,0:T(8,128)(2,1)S(1)}, u32[]{:S(2)}, u32[]{:S(2)}) collective-permute-start(bf16[256,256]{1,0:T(8,128)(2,1)S(1)} %get-tuple-element.8), channel_id=1, source_target_pairs={{0,8},{2,10},{4,12},{6,14},{8,0},{10,2},{12,4},{14,6},{16,24},{18,... | collective-permute-start | bytes 393224 | tf_op jit(solution)/shard_map/ppermute | solution.py:11
  91.7 6.7 copy-start.7
  91.7 17.2 %collective-permute-start.11 = (bf16[256,256]{1,0:T(8,128)(2,1)S(1)}, bf16[256,256]{1,0:T(8,128)(2,1)S(1)}, u32[]{:S(2)}, u32[]{:S(2)}) collective-permute-start(bf16[256,256]{1,0:T(8,128)(2,1)S(1)} %get-tuple-element.7), channel_id=1, source_target_pairs={{0,16},{2,18},{4,20},{6,22},{8,24},{10,26},{12,28},{14,30},{16,0},... | collective-permute-start | bytes 393224 | tf_op jit(solution)/shard_map/ppermute | solution.py:11
  93.5 11.5 collective-permute-start.6
  94.9 12.8 collective-permute-start.8
  99.6 1166.1 %collective-permute-start.5 = (bf16[256,256]{1,0:T(8,128)(2,1)}, bf16[256,256]{1,0:T(8,128)(2,1)S(1)}, u32[]{:S(2)}, u32[]{:S(2)}) collective-permute-start(bf16[256,256]{1,0:T(8,128)(2,1)} %get-tuple-element.5), channel_id=1, source_target_pairs={{0,2},{2,0},{4,6},{6,4},{8,10},{10,8},{12,14},{14,12},{16,18},{18,... | collective-permute-start | bytes 393224 | tf_op jit(solution)/shard_map/ppermute | solution.py:11
  105.0 12.3 collective-permute-start.10
  106.8 1158.9 %collective-permute-start.4 = (bf16[768,256]{1,0:T(8,128)(2,1)S(1)}, bf16[768,256]{1,0:T(8,128)(2,1)}, u32[]{:S(2)}, u32[]{:S(2)}) collective-permute-start(bf16[768,256]{1,0:T(8,128)(2,1)S(1)} %all_to_all.59), channel_id=1, source_target_pairs={{0,2},{2,0},{4,6},{6,4},{8,10},{10,8},{12,14},{14,12},{16,18},{18,... | collective-permute-start | bytes 1179656 | tf_op jit(solution)/shard_map/ppermute | solution.py:11
  1263.0 2.7 copy-start.3
  1270.4 35.5 %all-to-all-start.3 = ((bf16[128,6,256]{2,1,0:T(8,128)(2,1)}), bf16[128,6,256]{2,1,0:T(8,128)(2,1)S(1)}, u32[]{:S(2)}, u32[]{:S(2)}) async-start(bf16[128,6,256]{2,1,0:T(8,128)(2,1)} %all_to_all.64), calls=%async_computation.3 | async-start | bytes 1048576 | tf_op jit(solution)/shard_map/all_to_all | solution.py:78
  1286.4 17.9 %reduce-scatter.11.cloned.1.call-start = ((), (), s32[]{:S(2)}) async-start(), calls=%async_computation.9 | async-start | bytes 196608 | tf_op jit(solution)/shard_map/reduce_scatter | solution.py:74
  1287.7 1.3 copy-start.1
  1287.8 1.4 copy-start.2
  1305.9 13.9 %copy-start.5 = (bf16[6,32768]{1,0:T(8,128)(2,1)S(1)}, bf16[6,32768]{1,0:T(8,128)(2,1)}, u32[]{:S(2)}) copy-start(bf16[6,32768]{1,0:T(8,128)(2,1)} %param.5) | copy-start | bytes 1179652
  1305.9 33.4 %all-to-all-start.2 = ((bf16[128,6,256]{2,1,0:T(8,128)(2,1)}), bf16[128,6,256]{2,1,0:T(8,128)(2,1)S(1)}, u32[]{:S(2)}, u32[]{:S(2)}) async-start(bf16[128,6,256]{2,1,0:T(8,128)(2,1)} %all_to_all.60), calls=%async_computation.2 | async-start | bytes 1048576 | tf_op jit(solution)/shard_map/all_to_all | solution.py:52
Sparse Core Ops, SparseCore 0:
  84.0 9.1 reduce-scatter.8
  98.7 822.8 reduce-scatter.14
  1265.8 13.9 reduce-scatter.12
  1290.0 14.3 reduce-scatter.10
where the time goes:
time: 1350 us
  waiting for transfers between devices  865 us (64%)
  blocking collectives  372 us (28%)
  starting transfers between devices  52.9 us (4%)
  matrix products  20.3 us (2%)
  between operations  14.1 us (1%)
  local copies, waits for them, and re-layouts  14 us (1%)
    unnamed x6, waiting for transfers between devices  801 us
    all_gather x1, blocking collectives, reduce_latents(): full = lax.all_gather(part.astype(jnp.bfloat16), 'hid', axis=0, tiled=True)  338 us
    all_to_all x1, blocking collectives, on_device(): lax.all_to_all(act_tok, 'hid', split_axis=1, concat_axis=0, tiled=True)  33.9 us
  transfers between devices with their start and end apart: 19, of which 6 were waited for; matrix products, arithmetic and copies ran while one was open for 3% of the time, Pallas kernels for 0%

commit v1 on v0

--- a/solution.py
+++ b/solution.py
@@ -20,7 +20,10 @@
     rows, wide = both.shape
     flat = both.reshape(rows * wide // 128, 128)
     part = lax.psum_scatter(flat, "hid", scatter_dimension=0, tiled=True)
-    full = lax.all_gather(part.astype(jnp.bfloat16), "hid", axis=0, tiled=True)
+    full = jnp.concatenate(
+        lax.all_to_all(jnp.stack([part.astype(jnp.bfloat16)] * lax.axis_size("hid")), "hid", 0, 0),
+        axis=0,
+    )
     full = full.reshape(rows, wide)
     return (full[:, : wide // 2], full[:, wide // 2 :])
 

time: 1350 us -> 1030 us (0.76)
  blocking collectives: 372 us -> 0 us
  starting transfers between devices: 52.9 us -> 81 us
  waiting for transfers between devices: 865 us -> 880 us
    all_gather x1 -> x0, blocking collectives: 338 us -> none  [reduce_latents(): full = lax.all_gather(part.astype(jnp.bfloat16), 'hid', axis=0, tiled=True)]
    all_to_all x1 -> x0, blocking collectives: 33.9 us -> none  [on_device(): lax.all_to_all(act_tok, 'hid', split_axis=1, concat_axis=0, tiled=True)]
    all_to_all x0 -> x2, starting transfers between devices: none -> 18.9 us  [the longest x1 11.5 us: reduce_latents(): lax.all_to_all(jnp.stack([part.astype(jnp.bfloat16)] * lax.axis_size('hid...]
    ppermute x12, waiting for transfers between devices: 13.2 us -> 31.5 us  [swapped(): lax.ppermute(x, axis, [(i, i ^ 1 << stride) for i in range(lax.axis_size(...]
    unnamed x6, waiting for transfers between devices: 801 us -> 783 us
    all_to_all x0 -> x2, waiting for transfers between devices: none -> 17.8 us  [the longest x1 17.8 us: on_device(): lax.all_to_all(act_tok, 'hid', split_axis=1, concat_axis=0, tiled=True)]
  transfers between devices with their start and end apart: 19 -> 21, of which waited for: 6 -> 9; matrix products, arithmetic and copies ran while one was open for 3% -> 4% of each run, Pallas kernels for 0% -> 0%
where the time goes in v1:
time: 1030 us; the launch traced here: 1020 us
  waiting for transfers between devices  880 us (85%)
  starting transfers between devices  81 us (8%)
  matrix products  24.7 us (2%)
  between operations  16 us (2%)
  local copies, waits for them, and re-layouts  13.4 us (1%)
    unnamed x6, waiting for transfers between devices  783 us
    ppermute x12, waiting for transfers between devices, swapped(): lax.ppermute(x, axis, [(i, i ^ 1 << stride) for i in range(lax.axis_size(...  31.5 us
  transfers between devices with their start and end apart: 21, of which 9 were waited for; matrix products, arithmetic and copies ran while one was open for 4% of the time, Pallas kernels for 0%

profile of v1, /device:TPU:32, one launch (start us, length us, event | category | flops | bytes accessed | tf_op | source)
XLA Modules:
  0.0 1024.8 jit_solution(8134420153605740223)
XLA Ops:
  8.0 15.1 %all-to-all-start.1 = ((bf16[6,128,256]{2,0,1:T(8,128)(2,1)}), bf16[6,128,256]{2,0,1:T(8,128)(2,1)S(1)}, u32[]{:S(2)}, u32[]{:S(2)}) async-start(bf16[6,128,256]{2,0,1:T(8,128)(2,1)} %bitcast.92), calls=%async_computation.1 | async-start | bytes 1048576 | tf_op jit(solution)/shard_map/all_to_all | solution.py:44
  23.2 1.2 fusion.22
  24.3 18.0 %all-to-all-done.1 = bf16[6,128,256]{2,0,1:T(8,128)(2,1)S(1)} async-done(((bf16[6,128,256]{2,0,1:T(8,128)(2,1)}), bf16[6,128,256]{2,0,1:T(8,128)(2,1)S(1)}, u32[]{:S(2)}, u32[]{:S(2)}) %all-to-all-start.1) | async-done | bytes 393248 | tf_op jit(solution)/shard_map/all_to_all | solution.py:44
  42.3 7.3 all-to-all-start
  49.8 17.8 %all-to-all-done = bf16[6,128,256]{2,0,1:T(8,128)(2,1)S(1)} async-done(((bf16[6,128,256]{2,0,1:T(8,128)(2,1)}), bf16[6,128,256]{2,0,1:T(8,128)(2,1)S(1)}, u32[]{:S(2)}, u32[]{:S(2)}) %all-to-all-start) | async-done | bytes 393248 | tf_op jit(solution)/shard_map/all_to_all | solution.py:40
  67.8 0.3 fusion.42
  68.1 0.3 fusion.41
  68.5 1.6 copy.19
  70.2 2.5 reshape.107
  72.7 1.0 collective-permute-start
  73.7 0.8 slice_bitcast_fusion.3
  74.5 2.4 collective-permute-start.7
  76.9 0.4 collective-permute-start.9
  77.3 2.0 collective-permute-start.11
  79.3 1.8 collective-permute-start.1
  81.1 1.1 copy.15
  82.2 2.0 fusion.13
  84.2 0.6 collective-permute-done
  84.8 1.2 collective-permute-start.2
  86.0 1.0 fusion.12
  87.0 6.7 collective-permute-done.1
  93.7 0.8 collective-permute-start.3
  94.5 1.0 fusion.11
  95.5 1.5 collective-permute-start.6
  97.0 1.0 fusion.10
  98.0 9.8 collective-permute-done.3
  107.8 2.6 collective-permute-start.8
  110.4 1.0 fusion.9
  111.4 783.3 %reduce-scatter.15.cloned.1.call-done = f32[24,128]{1,0:T(8,128)} async-done(((f32[3072,128]{1,0:T(8,128)}), f32[24,128]{1,0:T(8,128)}) %reduce-scatter.15.cloned.1.call-update) | async-done | bytes 12304
  894.7 0.7 convert_element_type.55
  895.4 1.0 stack.14
  896.4 11.5 %all-to-all-start.2 = ((bf16[128,24,128]{2,1,0:T(8,128)(2,1)}), bf16[128,24,128]{2,1,0:T(8,128)(2,1)S(1)}, u32[]{:S(2)}, u32[]{:S(2)}) async-start(bf16[128,24,128]{2,1,0:T(8,128)(2,1)} %stack.14), calls=%async_computation.2 | async-start | bytes 1572864 | tf_op jit(solution)/shard_map/all_to_all | solution.py:24
  908.0 2.3 multiply_convert_fusion
  910.4 1.2 fusion.38
  911.6 1.1 fusion.39
  912.7 1.2 fusion.40
  913.9 1.5 collective-permute-start.5
  915.3 2.4 collective-permute-start.10
  917.7 2.2 fusion.43
  919.9 0.6 collective-permute-start.4
  920.5 1.3 fusion.44
  921.8 14.3 %collective-permute-done.10 = bf16[768,256]{1,0:T(8,128)(2,1)S(1)} collective-permute-done((bf16[768,256]{1,0:T(8,128)(2,1)S(1)}, bf16[768,256]{1,0:T(8,128)(2,1)S(1)}, u32[]{:S(2)}, u32[]{:S(2)}) %collective-permute-start.10) | collective-permute-done | bytes 393248 | tf_op jit(solution)/shard_map/ppermute | solution.py:11
  936.2 2.1 fusion.45
  938.2 1.9 convert_element_type.63
  940.1 0.5 reshape_reshape.3
  940.6 0.3 fusion.29
  940.9 2.1 convolution_add_fusion.1
  943.0 0.3 fusion.14
  943.3 0.8 copy.22
  944.1 2.6 fusion.8
  946.7 1.9 all_to_all.68
  948.6 15.0 %all-to-all-start.4 = ((bf16[128,6,256]{2,1,0:T(8,128)(2,1)}), bf16[128,6,256]{2,1,0:T(8,128)(2,1)S(1)}, u32[]{:S(2)}, u32[]{:S(2)}) async-start(bf16[128,6,256]{2,1,0:T(8,128)(2,1)} %all_to_all.68), calls=%async_computation.4 | async-start | bytes 1048576 | tf_op jit(solution)/shard_map/all_to_all | solution.py:81
  963.7 1.0 fusion.15
  965.0 1.3 convolution_add_fusion.3
  966.5 1.2 fusion.7
  967.7 0.9 all_to_all.64
  968.7 0.9 copy.23
  969.6 0.7 convert_element_type.65
  970.3 11.1 %reduce-scatter.11.cloned.1.call-done = bf16[128,256]{1,0:T(8,128)(2,1)} async-done(((bf16[256,256]{1,0:T(8,128)(2,1)}), bf16[128,256]{1,0:T(8,128)(2,1)}) %reduce-scatter.11.cloned.1.call-update) | async-done | bytes 65552 | tf_op jit(solution)/shard_map/reduce_scatter | solution.py:77
  981.4 1.5 convert_element_type.67
  982.9 13.8 %all-to-all-start.3 = ((bf16[128,6,256]{2,1,0:T(8,128)(2,1)}), bf16[128,6,256]{2,1,0:T(8,128)(2,1)S(1)}, u32[]{:S(2)}, u32[]{:S(2)}) async-start(bf16[128,6,256]{2,1,0:T(8,128)(2,1)} %all_to_all.64), calls=%async_computation.3 | async-start | bytes 1048576 | tf_op jit(solution)/shard_map/all_to_all | solution.py:55
  996.8 1.5 fusion.18
  998.3 18.1 %all-to-all-done.3 = bf16[128,6,256]{2,1,0:T(8,128)(2,1)S(1)} async-done(((bf16[128,6,256]{2,1,0:T(8,128)(2,1)}), bf16[128,6,256]{2,1,0:T(8,128)(2,1)S(1)}, u32[]{:S(2)}, u32[]{:S(2)}) %all-to-all-start.3) | async-done | bytes 393248 | tf_op jit(solution)/shard_map/all_to_all | solution.py:55
  1016.4 0.8 copy.33
  (53 shorter events, 1.3 us)
Async XLA Ops:
  8.0 60.1 %copy-start = (bf16[256,256]{1,0:T(8,128)(2,1)S(1)}, bf16[256,256]{1,0:T(8,128)(2,1)}, u32[]{:S(2)}) copy-start(bf16[256,256]{1,0:T(8,128)(2,1)} %param.7) | copy-start | bytes 393220
  8.0 15.2 %copy-start.8 = (bf16[6,32768]{1,0:T(8,128)(2,1)S(1)}, bf16[6,32768]{1,0:T(8,128)(2,1)}, u32[]{:S(2)}) copy-start(bf16[6,32768]{1,0:T(8,128)(2,1)} %param.5) | copy-start | bytes 1179652
  8.0 34.3 %all-to-all-start.1 = ((bf16[6,128,256]{2,0,1:T(8,128)(2,1)}), bf16[6,128,256]{2,0,1:T(8,128)(2,1)S(1)}, u32[]{:S(2)}, u32[]{:S(2)}) async-start(bf16[6,128,256]{2,0,1:T(8,128)(2,1)} %bitcast.92), calls=%async_computation.1 | async-start | bytes 1048576 | tf_op jit(solution)/shard_map/all_to_all | solution.py:44
  42.3 25.5 %copy-start.6 = (bf16[6,128,256]{2,0,1:T(8,128)(2,1)}, bf16[6,128,256]{2,0,1:T(8,128)(2,1)S(1)}, u32[]{:S(2)}) copy-start(bf16[6,128,256]{2,0,1:T(8,128)(2,1)S(1)} %all-to-all-done.1) | copy-start | bytes 1179652
  42.3 25.5 %copy-start.12 = (bf16[256,256]{1,0:T(8,128)(2,1)S(1)}, bf16[256,256]{1,0:T(8,128)(2,1)}, u32[]{:S(2)}) copy-start(bf16[256,256]{1,0:T(8,128)(2,1)} %param.8) | copy-start | bytes 393220
  42.3 25.3 %all-to-all-start = ((bf16[6,128,256]{2,0,1:T(8,128)(2,1)}), bf16[6,128,256]{2,0,1:T(8,128)(2,1)S(1)}, u32[]{:S(2)}, u32[]{:S(2)}) async-start(bf16[6,128,256]{2,0,1:T(8,128)(2,1)} %bitcast), calls=%async_computation | async-start | bytes 1048576 | tf_op jit(solution)/shard_map/all_to_all | solution.py:40
  49.6 845.1 %reduce-scatter.15.cloned.1.call-start = ((), (), s32[]{:S(2)}) async-start(), calls=%async_computation.12 | async-start | bytes 1585152
  72.7 1.1 copy-start.5
  72.7 9.5 copy-start.7
  72.7 12.1 %collective-permute-start = (bf16[768,256]{1,0:T(8,128)(2,1)S(1)}, bf16[768,256]{1,0:T(8,128)(2,1)S(1)}, u32[]{:S(2)}, u32[]{:S(2)}) collective-permute-start(bf16[768,256]{1,0:T(8,128)(2,1)S(1)} %all_to_all.58), channel_id=1, source_target_pairs={{0,2},{2,0},{4,6},{6,4},{8,10},{10,8},{12,14},{14,12},{16,18},{18,... | collective-permute-start | bytes 1179656 | tf_op jit(solution)/shard_map/ppermute | solution.py:11
  74.5 839.3 %collective-permute-start.7 = (bf16[256,256]{1,0:T(8,128)(2,1)}, bf16[256,256]{1,0:T(8,128)(2,1)}, u32[]{:S(2)}, u32[]{:S(2)}) collective-permute-start(bf16[256,256]{1,0:T(8,128)(2,1)} %get-tuple-element.6), channel_id=1, source_target_pairs={{0,4},{2,6},{4,0},{6,2},{8,12},{10,14},{12,8},{14,10},{16,20},{18,... | collective-permute-start | bytes 393224 | tf_op jit(solution)/shard_map/ppermute | solution.py:11
  76.9 843.0 %collective-permute-start.9 = (bf16[256,256]{1,0:T(8,128)(2,1)}, bf16[256,256]{1,0:T(8,128)(2,1)}, u32[]{:S(2)}, u32[]{:S(2)}) collective-permute-start(bf16[256,256]{1,0:T(8,128)(2,1)} %get-tuple-element.8), channel_id=1, source_target_pairs={{0,8},{2,10},{4,12},{6,14},{8,0},{10,2},{12,4},{14,6},{16,24},{18,... | collective-permute-start | bytes 393224 | tf_op jit(solution)/shard_map/ppermute | solution.py:11
  77.3 844.5 %collective-permute-start.11 = (bf16[256,256]{1,0:T(8,128)(2,1)}, bf16[256,256]{1,0:T(8,128)(2,1)}, u32[]{:S(2)}, u32[]{:S(2)}) collective-permute-start(bf16[256,256]{1,0:T(8,128)(2,1)} %get-tuple-element.7), channel_id=1, source_target_pairs={{0,16},{2,18},{4,20},{6,22},{8,24},{10,26},{12,28},{14,30},{16,0},... | collective-permute-start | bytes 393224 | tf_op jit(solution)/shard_map/ppermute | solution.py:11
  79.3 14.3 %collective-permute-start.1 = (bf16[768,256]{1,0:T(8,128)(2,1)S(1)}, bf16[768,256]{1,0:T(8,128)(2,1)S(1)}, u32[]{:S(2)}, u32[]{:S(2)}) collective-permute-start(bf16[768,256]{1,0:T(8,128)(2,1)S(1)} %all_to_all.58), channel_id=1, source_target_pairs={{0,4},{2,6},{4,0},{6,2},{8,12},{10,14},{12,8},{14,10},{16,20},{18,... | collective-permute-start | bytes 1179656 | tf_op jit(solution)/shard_map/ppermute | solution.py:11
  84.8 13.2 %copy-start.10 = (bf16[768,256]{1,0:T(8,128)(2,1)}, bf16[768,256]{1,0:T(8,128)(2,1)S(1)}, u32[]{:S(2)}) copy-start(bf16[768,256]{1,0:T(8,128)(2,1)S(1)} %collective-permute-done) | copy-start | bytes 1179652
  84.8 10.7 %collective-permute-start.2 = (bf16[768,256]{1,0:T(8,128)(2,1)S(1)}, bf16[768,256]{1,0:T(8,128)(2,1)S(1)}, u32[]{:S(2)}, u32[]{:S(2)}) collective-permute-start(bf16[768,256]{1,0:T(8,128)(2,1)S(1)} %all_to_all.58), channel_id=1, source_target_pairs={{0,8},{2,10},{4,12},{6,14},{8,0},{10,2},{12,4},{14,6},{16,24},{18,... | collective-permute-start | bytes 1179656 | tf_op jit(solution)/shard_map/ppermute | solution.py:11
  93.7 14.2 %collective-permute-start.3 = (bf16[768,256]{1,0:T(8,128)(2,1)S(1)}, bf16[768,256]{1,0:T(8,128)(2,1)S(1)}, u32[]{:S(2)}, u32[]{:S(2)}) collective-permute-start(bf16[768,256]{1,0:T(8,128)(2,1)S(1)} %all_to_all.58), channel_id=1, source_target_pairs={{0,16},{2,18},{4,20},{6,22},{8,24},{10,26},{12,28},{14,30},{16,0},... | collective-permute-start | bytes 1179656 | tf_op jit(solution)/shard_map/ppermute | solution.py:11
  95.5 819.9 %collective-permute-start.6 = (bf16[768,256]{1,0:T(8,128)(2,1)S(1)}, bf16[768,256]{1,0:T(8,128)(2,1)}, u32[]{:S(2)}, u32[]{:S(2)}) collective-permute-start(bf16[768,256]{1,0:T(8,128)(2,1)S(1)} %all_to_all.62), channel_id=1, source_target_pairs={{0,4},{2,6},{4,0},{6,2},{8,12},{10,14},{12,8},{14,10},{16,20},{18,... | collective-permute-start | bytes 1179656 | tf_op jit(solution)/shard_map/ppermute | solution.py:11
  107.8 812.6 %collective-permute-start.8 = (bf16[768,256]{1,0:T(8,128)(2,1)S(1)}, bf16[768,256]{1,0:T(8,128)(2,1)}, u32[]{:S(2)}, u32[]{:S(2)}) collective-permute-start(bf16[768,256]{1,0:T(8,128)(2,1)S(1)} %all_to_all.62), channel_id=1, source_target_pairs={{0,8},{2,10},{4,12},{6,14},{8,0},{10,2},{12,4},{14,6},{16,24},{18,... | collective-permute-start | bytes 1179656 | tf_op jit(solution)/shard_map/ppermute | solution.py:11
  896.4 43.7 %all-to-all-start.2 = ((bf16[128,24,128]{2,1,0:T(8,128)(2,1)}), bf16[128,24,128]{2,1,0:T(8,128)(2,1)S(1)}, u32[]{:S(2)}, u32[]{:S(2)}) async-start(bf16[128,24,128]{2,1,0:T(8,128)(2,1)} %stack.14), calls=%async_computation.2 | async-start | bytes 1572864 | tf_op jit(solution)/shard_map/all_to_all | solution.py:24
  908.0 30.3 %reduce-scatter.9.cloned.1.call-start = ((), (), s32[]{:S(2)}) async-start(), calls=%async_computation.9 | async-start | bytes 983040 | tf_op jit(solution)/shard_map/reduce_scatter | solution.py:71
  910.3 58.3 %reduce-scatter.13.cloned.1.call-start = ((), (), s32[]{:S(2)}) async-start(), calls=%async_computation.11 | async-start | bytes 196608
  913.9 30.2 %collective-permute-start.5 = (bf16[256,256]{1,0:T(8,128)(2,1)}, bf16[256,256]{1,0:T(8,128)(2,1)S(1)}, u32[]{:S(2)}, u32[]{:S(2)}) collective-permute-start(bf16[256,256]{1,0:T(8,128)(2,1)} %get-tuple-element.5), channel_id=1, source_target_pairs={{0,2},{2,0},{4,6},{6,4},{8,10},{10,8},{12,14},{14,12},{16,18},{18,... | collective-permute-start | bytes 393224 | tf_op jit(solution)/shard_map/ppermute | solution.py:11
  915.3 20.8 %collective-permute-start.10 = (bf16[768,256]{1,0:T(8,128)(2,1)S(1)}, bf16[768,256]{1,0:T(8,128)(2,1)S(1)}, u32[]{:S(2)}, u32[]{:S(2)}) collective-permute-start(bf16[768,256]{1,0:T(8,128)(2,1)S(1)} %all_to_all.62), channel_id=1, source_target_pairs={{0,16},{2,18},{4,20},{6,22},{8,24},{10,26},{12,28},{14,30},{16,0},... | collective-permute-start | bytes 1179656 | tf_op jit(solution)/shard_map/ppermute | solution.py:11
  919.9 24.2 %collective-permute-start.4 = (bf16[768,256]{1,0:T(8,128)(2,1)S(1)}, bf16[768,256]{1,0:T(8,128)(2,1)}, u32[]{:S(2)}, u32[]{:S(2)}) collective-permute-start(bf16[768,256]{1,0:T(8,128)(2,1)S(1)} %all_to_all.62), channel_id=1, source_target_pairs={{0,2},{2,0},{4,6},{6,4},{8,10},{10,8},{12,14},{14,12},{16,18},{18,... | collective-permute-start | bytes 1179656 | tf_op jit(solution)/shard_map/ppermute | solution.py:11
  943.0 1.1 copy-start.4
  948.6 16.1 %copy-start.13 = (bf16[256,256]{1,0:T(8,128)(2,1)S(1)}, bf16[256,256]{1,0:T(8,128)(2,1)}, u32[]{:S(2)}) copy-start(bf16[256,256]{1,0:T(8,128)(2,1)} %param.8) | copy-start | bytes 393220
  948.6 34.3 %all-to-all-start.4 = ((bf16[128,6,256]{2,1,0:T(8,128)(2,1)}), bf16[128,6,256]{2,1,0:T(8,128)(2,1)S(1)}, u32[]{:S(2)}, u32[]{:S(2)}) async-start(bf16[128,6,256]{2,1,0:T(8,128)(2,1)} %all_to_all.68), calls=%async_computation.4 | async-start | bytes 1048576 | tf_op jit(solution)/shard_map/all_to_all | solution.py:81
  963.6 17.7 %reduce-scatter.11.cloned.1.call-start = ((), (), s32[]{:S(2)}) async-start(), calls=%async_computation.10 | async-start | bytes 196608 | tf_op jit(solution)/shard_map/reduce_scatter | solution.py:77
  964.7 1.6 copy-start.3
  964.9 1.4 copy-start.1
  965.0 1.5 copy-start.2
  965.0 1.6 copy-start.11
  982.9 13.9 %copy-start.9 = (bf16[6,32768]{1,0:T(8,128)(2,1)S(1)}, bf16[6,32768]{1,0:T(8,128)(2,1)}, u32[]{:S(2)}) copy-start(bf16[6,32768]{1,0:T(8,128)(2,1)} %param.5) | copy-start | bytes 1179652
  982.9 33.5 %all-to-all-start.3 = ((bf16[128,6,256]{2,1,0:T(8,128)(2,1)}), bf16[128,6,256]{2,1,0:T(8,128)(2,1)S(1)}, u32[]{:S(2)}, u32[]{:S(2)}) async-start(bf16[128,6,256]{2,1,0:T(8,128)(2,1)} %all_to_all.64), calls=%async_computation.3 | async-start | bytes 1048576 | tf_op jit(solution)/shard_map/all_to_all | solution.py:55
Sparse Core Ops, SparseCore 0:
  72.8 821.8 reduce-scatter.14
Sparse Core Ops, SparseCore 1:
  911.5 14.6 reduce-scatter.8
  944.2 15.2 reduce-scatter.12
  967.1 14.2 reduce-scatter.10
